TPU v7x, 256 devices: a whole 4x4x8 slice. The times are simulated.
256 devices in a mesh: dp: 32 (over z, x_hi, core), tensor: 8 (over x_lo, y).
Axes of the slice: x: 4 (x_hi: 2, x_lo: 2; x = x_hi * 2 + x_lo), y: 4, z: 8, core: 2. Of those that a mesh axis runs over, the one named last changes fastest.
Arguments:
- hidden: bfloat16 [16384, 14336], P('dp', 'tensor'), may hold values from -76 to 76
- base_weight: bfloat16 [14336, 4096], P('tensor', 'dp'), may hold values from -0.046875 to 0.046875
- adapter_in: bfloat16 [256, 14336], P(None, 'tensor'), may hold values from -0.046875 to 0.046875
- adapter_out: bfloat16 [256, 4096], P(None, 'tensor'), may hold values from -0.375 to 0.375
- cotangent: bfloat16 [16384, 4096], P('dp', 'tensor'), may hold values from -0.046875 to 0.046875
Outputs:
- output: bfloat16 [16384, 4096], P('dp', 'tensor')
- grad_in: float32 [256, 14336], P('dp', 'tensor')
- grad_out: float32 [256, 4096], P('dp', 'tensor')
All inputs are finite; a program needn't handle non-finite values.
Results may differ from a plain program's by a relative error of at most 0.0031.
Values may be sent and summed in bfloat16 or wider, within the bound.
A program may use at most 128 MiB of HBM per device.

v0:
```python
import jax
import jax.numpy as jnp
from jax import lax
from jax.sharding import PartitionSpec as P

adapter_scale = 4.0
exp_rate = 0.25
tiny_eps = 1e-06


def inverse_sinh(value):
    return jnp.log(value + jnp.sqrt(1.0 + value * value))


def shards(hidden, base_weight, adapter_in, adapter_out, cotangent):
    feature_count = hidden.shape[1] * lax.axis_size("tensor")
    contract_last = (((1,), (1,)), ((), ()))
    contract_first = (((0,), (0,)), ((), ()))
    square_part = jnp.sum(jnp.square(hidden.astype(jnp.float32)), axis=1)
    rank_part = lax.dot_general(
        hidden, adapter_in, contract_last, preferred_element_type=jnp.float32
    )
    square_sum, lorentz_raw = lax.psum((square_part, rank_part), "tensor")
    level = jnp.sqrt(square_sum / feature_count + tiny_eps)
    radius = exp_rate * level
    lift_factor = jnp.sinh(radius) / radius
    lorentz = lift_factor[:, None] * lorentz_raw
    norm_value = jnp.sqrt(jnp.sum(lorentz * lorentz, axis=1) + tiny_eps)
    phi_value = inverse_sinh(norm_value) / norm_value
    tangent = (phi_value[:, None] * lorentz).astype(jnp.bfloat16)
    partial_cols = jnp.dot(
        hidden,
        lax.all_gather(base_weight, "dp", axis=1, tiled=True),
        preferred_element_type=jnp.float32,
    )
    base_sum = lax.psum_scatter(partial_cols, "tensor", scatter_dimension=1, tiled=True)
    adapter_term = jnp.dot(tangent, adapter_out, preferred_element_type=jnp.float32)
    output = (base_sum + adapter_scale * adapter_term).astype(jnp.bfloat16)
    out_part = adapter_scale * lax.dot_general(
        tangent, cotangent, contract_first, preferred_element_type=jnp.float32
    )
    cotan_later = adapter_scale * lax.dot_general(
        cotangent, adapter_out, contract_last, preferred_element_type=jnp.float32
    )
    tangent_grad = lax.psum(cotan_later, "tensor")
    inner_value = jnp.sum(lorentz * tangent_grad, axis=1)
    coefficient = (1.0 / jnp.sqrt(1.0 + norm_value * norm_value) - phi_value) / (
        norm_value * norm_value
    )
    lorentz_grad = (
        phi_value[:, None] * tangent_grad + (coefficient * inner_value)[:, None] * lorentz
    )
    raw_grad = (lift_factor[:, None] * lorentz_grad).astype(jnp.bfloat16)
    in_part = lax.dot_general(raw_grad, hidden, contract_first, preferred_element_type=jnp.float32)
    grad_in, grad_out = (
        lax.psum_scatter(in_part, "dp", scatter_dimension=0, tiled=True),
        lax.psum_scatter(out_part, "dp", scatter_dimension=0, tiled=True),
    )
    return (output, grad_in, grad_out)


def solution(mesh):
    return jax.shard_map(
        shards,
        mesh=mesh,
        in_specs=(
            P("dp", "tensor"),
            P("tensor", "dp"),
            P(None, "tensor"),
            P(None, "tensor"),
            P("dp", "tensor"),
        ),
        out_specs=(P("dp", "tensor"), P("dp", "tensor"), P("dp", "tensor")),
        check_vma=False,
    )
```

profile of v0, /device:TPU:8, one launch (start us, length us, event | category | flops | bytes accessed | tf_op | source)
XLA Modules:
  0.0 506.5 jit_solution(1643194782338314883)
XLA Ops:
  8.0 0.0 all-gather.2.cloned.1.call-start
  8.1 0.7 all-gather.2.cloned.1.call-update
  8.7 0.0 all-reduce.3.cloned.1.call-start
  8.8 2.2 convolution_multiply_fusion.2
  11.0 3.1 fusion.12
  14.1 0.0 all-reduce.3.cloned.1.call-update
  14.2 0.0 reduce-scatter.4.cloned.1.call-start
  14.2 141.3 %all-gather.2.cloned.1.call-done = bf16[1792,4096]{1,0:T(8,128)(2,1)} async-done(((bf16[1792,128]{1,0:T(8,128)(2,1)}), bf16[1792,4096]{1,0:T(8,128)(2,1)}) %all-gather.2.cloned.1.call-update) | async-done | bytes 14680080 | tf_op jit(solution)/shard_map/all_gather | solution.py:33
  155.5 13.0 %fusion.11 = f32[512,4096]{1,0:T(8,128)} fusion(bf16[512,1792]{1,0:T(8,128)(2,1)S(1)} %copy-done.2, bf16[1792,4096]{1,0:T(8,128)(2,1)} %all-gather.2.cloned.1.call-done), kind=kOutput, calls=%fused_computation.25 | convolution fusion | flops 7516192768 | bytes 24903680 | tf_op jit(solution)/shard_map/dot_general | solution.py:31
  168.5 0.0 reduce-scatter.4.cloned.1.call-update
  168.5 0.0 reduce-scatter.8.cloned.1.call-start
  168.6 0.4 multiply_reduce_fusion
  169.0 16.6 %psum.21 = f32[512]{0:T(512)S(1)} all-reduce(f32[512]{0:T(512)S(1)} %multiply_reduce_fusion), channel_id=1, replica_groups=mesh['dp'=32,'tensor'=8] {'tensor'}, use_global_device_ids=true, to_apply=%region_2.0 | all-reduce | flops 512 | bytes 4096 | tf_op jit(solution)/shard_map/psum | solution.py:23
  185.7 0.0 all-reduce.3.cloned.1.call-done
  185.7 1.6 multiply_reduce_fusion.1
  187.3 2.6 convolution_multiply_fusion.1
  189.9 0.0 reduce-scatter.8.cloned.1.call-update
  190.0 0.0 reduce-scatter.6.cloned.1.call-start
  190.0 3.1 fusion.2
  193.2 0.0 reduce-scatter.6.cloned.1.call-update
  193.2 64.9 %reduce-scatter.4.cloned.1.call-done = f32[512,512]{1,0:T(8,128)} async-done(((f32[512,4096]{1,0:T(8,128)}), f32[512,512]{1,0:T(8,128)}) %reduce-scatter.4.cloned.1.call-update) | async-done | bytes 1048592 | tf_op jit(solution)/shard_map/reduce_scatter | solution.py:36
  258.1 2.4 fusion.1
  260.5 116.9 %reduce-scatter.8.cloned.1.call-done = f32[8,512]{1,0:T(8,128)} async-done(((f32[256,512]{1,0:T(8,128)}), f32[8,512]{1,0:T(8,128)}) %reduce-scatter.8.cloned.1.call-update) | async-done | bytes 16400 | tf_op jit(solution)/shard_map/reduce_scatter | solution.py:57
  377.3 121.6 %reduce-scatter.6.cloned.1.call-done = f32[8,1792]{1,0:T(8,128)} async-done(((f32[256,1792]{1,0:T(8,128)}), f32[8,1792]{1,0:T(8,128)}) %reduce-scatter.6.cloned.1.call-update) | async-done | bytes 57360 | tf_op jit(solution)/shard_map/reduce_scatter | solution.py:56
  (10 shorter events, 0.1 us)
Async XLA Ops:
  8.0 3.0 copy-start
  8.0 147.5 %all-gather.2.cloned.1.call-start = ((), (), s32[]{:S(2)}) async-start(), calls=%async_computation.3 | async-start | bytes 15138816 | tf_op jit(solution)/shard_map/all_gather | solution.py:33
  8.7 176.9 %all-reduce.3.cloned.1.call-start = ((), (), s32[]{:S(2)}) async-start(), calls=%async_computation.7 | async-start | bytes 2097152 | tf_op jit(solution)/shard_map/psum | solution.py:23
  11.0 144.5 %copy-start.2 = (bf16[512,1792]{1,0:T(8,128)(2,1)S(1)}, bf16[512,1792]{1,0:T(8,128)(2,1)}, u32[]{:S(2)}) copy-start(bf16[512,1792]{1,0:T(8,128)(2,1)} %param.5) | copy-start | bytes 5505028
  14.2 243.9 %reduce-scatter.4.cloned.1.call-start = ((), (), s32[]{:S(2)}) async-start(), calls=%async_computation.4 | async-start | bytes 9437184 | tf_op jit(solution)/shard_map/reduce_scatter | solution.py:36
  168.5 208.8 %reduce-scatter.8.cloned.1.call-start = ((), (), s32[]{:S(2)}) async-start(), calls=%async_computation.6 | async-start | bytes 540672 | tf_op jit(solution)/shard_map/reduce_scatter | solution.py:57
  185.7 4.3 copy-start.1
  190.0 308.9 %reduce-scatter.6.cloned.1.call-start = ((), (), s32[]{:S(2)}) async-start(), calls=%async_computation.5 | async-start | bytes 1892352 | tf_op jit(solution)/shard_map/reduce_scatter | solution.py:56
  193.2 64.9 %copy-start.3 = (bf16[256,512]{1,0:T(8,128)(2,1)S(1)}, bf16[256,512]{1,0:T(8,128)(2,1)}, u32[]{:S(2)}) copy-start(bf16[256,512]{1,0:T(8,128)(2,1)} %param.8) | copy-start | bytes 786436
Sparse Core Ops, SparseCore 0:
  11.4 144.0 all-gather.1
Sparse Core Ops, SparseCore 1:
  14.2 125.5 all-reduce.2
  168.6 89.4 reduce-scatter.3
  262.6 114.7 reduce-scatter.7
  382.6 116.2 reduce-scatter.5
where the time goes:
time: 507 us
  waiting for transfers between devices  445 us (88%)
  matrix products  26.5 us (5%)
  blocking collectives  16.6 us (3%)
  between operations  15.7 us (3%)
    all_gather x1, waiting for transfers between devices, shards(): lax.all_gather(base_weight, 'dp', axis=1, tiled=True)  141 us
    reduce_scatter x1, waiting for transfers between devices, shards(): lax.psum_scatter(in_part, 'dp', scatter_dimension=0, tiled=True)  122 us
    reduce_scatter x1, waiting for transfers between devices, shards(): lax.psum_scatter(out_part, 'dp', scatter_dimension=0, tiled=True)  117 us
    reduce_scatter x1, waiting for transfers between devices, shards(): lax.psum_scatter(partial_cols, 'tensor', scatter_dimension=1, tiled=True)  64.9 us
    psum x1, blocking collectives, shards(): square_sum, lorentz_raw = lax.psum((square_part, rank_part), 'tensor')  16.6 us
    dot_general x1, matrix products, shards(): jnp.dot(hidden, lax.all_gather(base_weight, 'dp', axis=1, tiled=True), pr...  13 us
  transfers between devices with their start and end apart: 5, of which 4 were waited for; matrix products, arithmetic and copies ran while one was open for 6% of the time, Pallas kernels for 0%

commit v1 on v0

--- a/solution.py
+++ b/solution.py
@@ -28,10 +28,16 @@
     norm_value = jnp.sqrt(jnp.sum(lorentz * lorentz, axis=1) + tiny_eps)
     phi_value = inverse_sinh(norm_value) / norm_value
     tangent = (phi_value[:, None] * lorentz).astype(jnp.bfloat16)
+
+    def _write_frame(my_tile, axis_key, pos_dim):
+        p_next = lax.axis_size(axis_key)
+        q_next = jnp.stack(p_next * [my_tile])
+        t_next = lax.all_to_all(q_next, axis_name=axis_key, split_axis=0, concat_axis=0)
+        block_out = jnp.concatenate(t_next, axis=pos_dim)
+        return block_out
+
     partial_cols = jnp.dot(
-        hidden,
-        lax.all_gather(base_weight, "dp", axis=1, tiled=True),
-        preferred_element_type=jnp.float32,
+        hidden, _write_frame(base_weight, "dp", 1), preferred_element_type=jnp.float32
     )
     base_sum = lax.psum_scatter(partial_cols, "tensor", scatter_dimension=1, tiled=True)
     adapter_term = jnp.dot(tangent, adapter_out, preferred_element_type=jnp.float32)

time: 507 us -> 700 us (1.38)
  waiting for transfers between devices: 445 us -> 623 us
  starting transfers between devices: 0.21 us -> 11.9 us
  local copies, waits for them, and re-layouts: 0.02 us -> 8.19 us
    all_to_all x0 -> x1, waiting for transfers between devices: none -> 312 us  [_write_frame(): lax.all_to_all(q_next, axis_name=axis_key, split_axis=0, concat_axis=0)]
    all_gather x1 -> x0, waiting for transfers between devices: 141 us -> none  [shards(): lax.all_gather(base_weight, 'dp', axis=1, tiled=True)]
    all_to_all x0 -> x1, starting transfers between devices: none -> 11.7 us  [_write_frame(): lax.all_to_all(q_next, axis_name=axis_key, split_axis=0, concat_axis=0)]
    reduce_scatter x1, waiting for transfers between devices: 64.9 us -> 73.3 us  [shards(): lax.psum_scatter(partial_cols, 'tensor', scatter_dimension=1, tiled=True)]
  transfers between devices with their start and end apart: 5 -> 5, of which waited for: 4 -> 4; matrix products, arithmetic and copies ran while one was open for 6% -> 4% of each run, Pallas kernels for 0% -> 0%
where the time goes in v1:
time: 700 us
  waiting for transfers between devices  623 us (89%)
  matrix products  23.8 us (3%)
  blocking collectives  16.4 us (2%)
  between operations  13.8 us (2%)
  starting transfers between devices  11.9 us (2%)
  local copies, waits for them, and re-layouts  8.19 us (1%)
    all_to_all x1, waiting for transfers between devices, _write_frame(): lax.all_to_all(q_next, axis_name=axis_key, split_axis=0, concat_axis=0)  312 us
    reduce_scatter x1, waiting for transfers between devices, shards(): lax.psum_scatter(in_part, 'dp', scatter_dimension=0, tiled=True)  121 us
    reduce_scatter x1, waiting for transfers between devices, shards(): lax.psum_scatter(out_part, 'dp', scatter_dimension=0, tiled=True)  117 us
    reduce_scatter x1, waiting for transfers between devices, shards(): lax.psum_scatter(partial_cols, 'tensor', scatter_dimension=1, tiled=True)  73.3 us
    psum x1, blocking collectives, shards(): square_sum, lorentz_raw = lax.psum((square_part, rank_part), 'tensor')  16.4 us
  transfers between devices with their start and end apart: 5, of which 4 were waited for; matrix products, arithmetic and copies ran while one was open for 4% of the time, Pallas kernels for 0%

profile of v1, /device:TPU:8, one launch (start us, length us, event | category | flops | bytes accessed | tf_op | source)
XLA Modules:
  0.0 699.5 jit_solution(1424321645614266320)
XLA Ops:
  7.2 1.3 copy.8
  8.5 6.9 stack.2
  15.4 11.7 %all-to-all-start = ((bf16[32,1792,128]{1,2,0:T(8,128)(2,1)}), bf16[32,1792,128]{1,2,0:T(8,128)(2,1)}, u32[]{:S(2)}, u32[]{:S(2)}) async-start(bf16[32,1792,128]{1,2,0:T(8,128)(2,1)} %stack.2), calls=%async_computation | async-start | bytes 29360128 | tf_op jit(solution)/shard_map/all_to_all | solution.py:35
  27.0 0.0 all-reduce.3.cloned.1.call-start
  27.1 1.1 convolution_multiply_fusion.2
  28.2 1.5 fusion.12
  29.7 0.0 all-reduce.3.cloned.1.call-update
  29.7 0.0 reduce-scatter.4.cloned.1.call-start
  29.8 311.6 %all-to-all-done = bf16[32,1792,128]{1,2,0:T(8,128)(2,1)} async-done(((bf16[32,1792,128]{1,2,0:T(8,128)(2,1)}), bf16[32,1792,128]{1,2,0:T(8,128)(2,1)}, u32[]{:S(2)}, u32[]{:S(2)}) %all-to-all-start) | async-done | bytes 14680096 | tf_op jit(solution)/shard_map/all_to_all | solution.py:35
  341.3 13.1 %fusion.11 = f32[512,4096]{1,0:T(8,128)} fusion(bf16[512,1792]{1,0:T(8,128)(2,1)S(1)} %copy-done.2, bf16[1792,4096]{0,1:T(8,128)(2,1)} %bitcast.1), kind=kOutput, calls=%fused_computation.25 | convolution fusion | flops 7516192768 | bytes 24903680 | tf_op jit(solution)/shard_map/dot_general | solution.py:39
  354.4 0.0 reduce-scatter.4.cloned.1.call-update
  354.4 0.0 reduce-scatter.8.cloned.1.call-start
  354.5 0.4 multiply_reduce_fusion
  354.9 16.4 %psum.21 = f32[512]{0:T(512)S(1)} all-reduce(f32[512]{0:T(512)S(1)} %multiply_reduce_fusion), channel_id=1, replica_groups=mesh['dp'=32,'tensor'=8] {'tensor'}, use_global_device_ids=true, to_apply=%region_2.0 | all-reduce | flops 512 | bytes 4096 | tf_op jit(solution)/shard_map/psum | solution.py:23
  371.3 0.0 all-reduce.3.cloned.1.call-done
  371.4 1.6 multiply_reduce_fusion.1
  373.0 2.6 convolution_multiply_fusion.1
  375.6 0.0 reduce-scatter.8.cloned.1.call-update
  375.6 0.0 reduce-scatter.6.cloned.1.call-start
  375.7 3.1 fusion.2
  378.9 73.3 %reduce-scatter.4.cloned.1.call-done = f32[512,512]{1,0:T(8,128)} async-done(((f32[512,4096]{1,0:T(8,128)}), f32[512,512]{1,0:T(8,128)}) %reduce-scatter.4.cloned.1.call-update) | async-done | bytes 1048592 | tf_op jit(solution)/shard_map/reduce_scatter | solution.py:42
  452.1 2.4 fusion.1
  454.5 117.0 %reduce-scatter.8.cloned.1.call-done = f32[8,512]{1,0:T(8,128)} async-done(((f32[256,512]{1,0:T(8,128)}), f32[8,512]{1,0:T(8,128)}) %reduce-scatter.8.cloned.1.call-update) | async-done | bytes 16400 | tf_op jit(solution)/shard_map/reduce_scatter | solution.py:63
  571.5 121.5 %reduce-scatter.6.cloned.1.call-done = f32[8,1792]{1,0:T(8,128)} async-done(((f32[256,1792]{1,0:T(8,128)}), f32[8,1792]{1,0:T(8,128)}) %reduce-scatter.6.cloned.1.call-update) | async-done | bytes 57360 | tf_op jit(solution)/shard_map/reduce_scatter | solution.py:62
  (13 shorter events, 0.1 us)
Async XLA Ops:
  7.2 21.1 %copy-start = (bf16[256,1792]{1,0:T(8,128)(2,1)S(1)}, bf16[256,1792]{1,0:T(8,128)(2,1)}, u32[]{:S(2)}) copy-start(bf16[256,1792]{1,0:T(8,128)(2,1)} %param.7) | copy-start | bytes 2752516
  15.3 11.8 %copy-start.3 = (bf16[512,512]{1,0:T(8,128)(2,1)S(1)}, bf16[512,512]{1,0:T(8,128)(2,1)}, u32[]{:S(2)}) copy-start(bf16[512,512]{1,0:T(8,128)(2,1)} %param.9) | copy-start | bytes 1572868
  15.3 11.8 %copy-start.4 = (bf16[256,512]{1,0:T(8,128)(2,1)S(1)}, bf16[256,512]{1,0:T(8,128)(2,1)}, u32[]{:S(2)}) copy-start(bf16[256,512]{1,0:T(8,128)(2,1)} %param.8) | copy-start | bytes 786436
  15.3 12.9 %copy-start.2 = (bf16[512,1792]{1,0:T(8,128)(2,1)S(1)}, bf16[512,1792]{1,0:T(8,128)(2,1)}, u32[]{:S(2)}) copy-start(bf16[512,1792]{1,0:T(8,128)(2,1)} %param.5) | copy-start | bytes 5505028
  15.4 326.0 %all-to-all-start = ((bf16[32,1792,128]{1,2,0:T(8,128)(2,1)}), bf16[32,1792,128]{1,2,0:T(8,128)(2,1)}, u32[]{:S(2)}, u32[]{:S(2)}) async-start(bf16[32,1792,128]{1,2,0:T(8,128)(2,1)} %stack.2), calls=%async_computation | async-start | bytes 29360128 | tf_op jit(solution)/shard_map/all_to_all | solution.py:35
  27.0 344.3 %all-reduce.3.cloned.1.call-start = ((), (), s32[]{:S(2)}) async-start(), calls=%async_computation.7 | async-start | bytes 2097152 | tf_op jit(solution)/shard_map/psum | solution.py:23
  29.7 422.4 %reduce-scatter.4.cloned.1.call-start = ((), (), s32[]{:S(2)}) async-start(), calls=%async_computation.4 | async-start | bytes 9437184 | tf_op jit(solution)/shard_map/reduce_scatter | solution.py:42
  354.4 217.1 %reduce-scatter.8.cloned.1.call-start = ((), (), s32[]{:S(2)}) async-start(), calls=%async_computation.6 | async-start | bytes 540672 | tf_op jit(solution)/shard_map/reduce_scatter | solution.py:63
  371.4 4.3 copy-start.1
  375.6 317.4 %reduce-scatter.6.cloned.1.call-start = ((), (), s32[]{:S(2)}) async-start(), calls=%async_computation.5 | async-start | bytes 1892352 | tf_op jit(solution)/shard_map/reduce_scatter | solution.py:62
Sparse Core Ops, SparseCore 0:
  31.1 107.4 all-reduce.2
  354.6 97.5 reduce-scatter.3
  456.7 114.7 reduce-scatter.7
  576.6 116.3 reduce-scatter.5
